TPU v7x, 32 devices: a whole 2x2x4 slice. The times are simulated.
32 devices in a mesh: gx: 8 (over z, x), gy: 4 (over y, core).
Axes of the slice: x: 2, y: 2, z: 4, core: 2. Of those that a mesh axis runs over, the one named last changes fastest.
Arguments:
- reference_scan: bfloat16 [128, 128, 2048], P('gx', 'gy'), may hold values from -6 to 6
- ref_gradient: bfloat16 [3, 128, 128, 2048], P(None, 'gx', 'gy'), may hold values from -6 to 6
- deformed_scan: bfloat16 [128, 128, 2048], P('gx', 'gy'), may hold values from -6 to 6
- interp_weights: bfloat16 [128, 128, 2048], P('gx', 'gy'), may hold values from 0 to 1
- sample_mask: int32 [128, 128, 2048], P('gx', 'gy'), may hold values from 0 to 1, as said below
- block_list: int32 [8, 16384], P('gx', 'gy'), may hold values from -1 to 8191, as said below
- offsets: int32 [2, 128, 128, 4], P(None, 'gx', 'gy'), may hold values from -4 to 4, as said below
Outputs:
- increment: float32 [3, 128, 128, 5], P(None, 'gx', 'gy')
- cg_residual: float32 [3, 128, 128, 5], P(None, 'gx', 'gy')
Inputs may be any that keep to these rules, and one draw needn't show every extreme that they name: sample_mask is 0 in every block of 128 voxels that its device's block_list does not name. `block_list`: each device's 4096 entries are first distinct local block indices, then -1 to the end; some device names exactly 4096 blocks. `offsets`: both ends of the range occur.
All inputs are finite; a program needn't handle non-finite values.
Results may differ from a plain program's by a relative error of at most 0.0045.
Values may be sent and summed in bfloat16 or wider, within the bound.
A program may use at most 320 MiB of HBM per device.

v0:
```python
import jax
import jax.numpy as jnp
from jax import lax
from jax.sharding import PartitionSpec as P

BOUND = 4
ITERS = 3
tikhonov = 8.0


def extended(value, sides, width):
    for axis, dim in sides:
        devices, length = (lax.axis_size(axis), value.shape[dim])
        up = [(i, (i + 1) % devices) for i in range(devices - 1)]
        down = [(j, i) for i, j in up]
        last = lax.slice_in_dim(value, length - width, length, axis=dim)
        first = lax.slice_in_dim(value, 0, width, axis=dim)
        before = lax.ppermute(last, axis, up)
        after = lax.ppermute(first, axis, down)
        value = jnp.concatenate([before, value, after], axis=dim)
    return value


def from_behind(block, axis, distance):
    devices = range(lax.axis_size(axis))
    route = [(i - distance, i) for i in devices if i - distance in devices]
    return lax.ppermute(block, axis, route)


def shape_table():
    voxel = jnp.arange(512)
    coords = [
        ((voxel // 64).astype(jnp.float32) + 0.5) / 8.0,
        ((voxel // 8 % 8).astype(jnp.float32) + 0.5) / 8.0,
        ((voxel % 8).astype(jnp.float32) + 0.5) / 8.0,
    ]
    rows = []
    for node in range(8):
        bits = [node >> 2 & 1, node >> 1 & 1, node & 1]
        value = jnp.ones((512,), jnp.float32)
        for axis_pos in range(3):
            value = value * (coords[axis_pos] if bits[axis_pos] else 1.0 - coords[axis_pos])
        rows.append(value)
    return jnp.transpose(jnp.stack(rows).reshape(8, 4, 128), (1, 0, 2))


def block_terms(grad_rows, resid_rows, mask_rows, kinds, table):
    onehot = (kinds[:, None] == jnp.arange(4)[None, :]).astype(jnp.float32)
    shapes = jnp.einsum("bk,knv->bnv", onehot, table, precision=lax.Precision.HIGHEST)
    product = shapes[:, :, None, :] * grad_rows[:, None, :, :].astype(jnp.float32)
    jacobian = product.reshape(kinds.shape[0], 24, 128).astype(jnp.bfloat16)
    weighted = jacobian * mask_rows[:, None, :]
    hessian = jnp.einsum("bdv,bev->bde", weighted, jacobian, preferred_element_type=jnp.float32)
    gradient = jnp.einsum("bdv,bv->bd", weighted, resid_rows, preferred_element_type=jnp.float32)
    return (hessian, gradient)


def run_groups(grad_rows, resid_rows, mask_rows, kinds, table):
    count = kinds.shape[0]
    groups = 4
    packed = (
        grad_rows.reshape((groups, count // groups) + grad_rows.shape[1:]),
        resid_rows.reshape(groups, count // groups, 128),
        mask_rows.reshape(groups, count // groups, 128),
        kinds.reshape(groups, count // groups),
    )
    hessian, gradient = lax.map(
        lambda parts: block_terms(parts[0], parts[1], parts[2], parts[3], table), packed
    )
    return (hessian.reshape(count, 24, 24), gradient.reshape(count, 24))


def per_device(
    reference_scan, ref_gradient, deformed_scan, interp_weights, sample_mask, block_list, offsets
):
    tile_x, tile_y, column = reference_scan.shape
    elem_depth = column // 512
    padded = extended(deformed_scan, (("gx", 0), ("gy", 1)), BOUND + 1)
    margin = BOUND + 1
    span_y = padded.shape[1]
    flat_scan = padded.reshape(padded.shape[0] * span_y, elem_depth, 512)
    pos_x = jnp.arange(tile_x)[:, None, None]
    pos_y = jnp.arange(tile_y)[None, :, None]
    source = (pos_x + offsets[0] + margin) * span_y + pos_y + offsets[1] + margin
    layer = jnp.broadcast_to(jnp.arange(elem_depth)[None, None, :], source.shape)
    near = flat_scan[source, layer].astype(jnp.float32)
    far = flat_scan[source + span_y, layer].astype(jnp.float32)
    weights = interp_weights.reshape(tile_x, tile_y, elem_depth, 512).astype(jnp.float32)
    warped = weights * near + (1.0 - weights) * far
    residual_image = (
        reference_scan.reshape(tile_x, tile_y, elem_depth, 512).astype(jnp.float32) - warped
    ).astype(jnp.bfloat16)
    local_blocks = tile_x * tile_y * elem_depth * 4
    elements = local_blocks // 4
    grad_blocks = jnp.moveaxis(ref_gradient.reshape(3, local_blocks, 128), 0, 1)
    resid_blocks = residual_image.reshape(local_blocks, 128)
    mask_blocks = sample_mask.reshape(local_blocks, 128)
    entries = block_list.reshape(-1)
    listed = entries >= 0
    safe = jnp.maximum(entries, 0)
    table = shape_table()
    marks = jnp.zeros((local_blocks,), jnp.bfloat16).at[safe].add(listed.astype(jnp.bfloat16))
    mask_rows = mask_blocks.astype(jnp.bfloat16) * marks[:, None]
    hessian, gradient = run_groups(
        grad_blocks, resid_blocks, mask_rows, jnp.arange(local_blocks) % 4, table
    )
    elem_hess = hessian.reshape(elements, 4, 24, 24).sum(axis=1)
    elem_load = gradient.reshape(elements, 4, 24).sum(axis=1)
    stiffness = jnp.transpose(elem_hess, (1, 2, 0))
    loads = jnp.transpose(elem_load, (1, 0))

    def spread(field):
        upper_x = from_behind(field[:, :1], "gx", -1)
        wide = jnp.concatenate([field, upper_x], axis=1)
        upper_y = from_behind(wide[:, :, :1], "gy", -1)
        wide = jnp.concatenate([wide, upper_y], axis=2)
        pieces = []
        for node in range(8):
            i_bit, j_bit, l_bit = (node >> 2 & 1, node >> 1 & 1, node & 1)
            pieces.append(
                wide[:, i_bit : i_bit + tile_x, j_bit : j_bit + tile_y, l_bit : l_bit + elem_depth]
            )
        return jnp.stack(pieces).reshape(24, elements)

    def collect(values):
        parts = values.reshape(8, 3, tile_x, tile_y, elem_depth)
        total = jnp.zeros((3, tile_x + 1, tile_y + 1, elem_depth + 1), jnp.float32)
        for node in range(8):
            i_bit, j_bit, l_bit = (node >> 2 & 1, node >> 1 & 1, node & 1)
            total = total + jnp.pad(
                parts[node], ((0, 0), (i_bit, 1 - i_bit), (j_bit, 1 - j_bit), (l_bit, 1 - l_bit))
            )
        passed_y = from_behind(total[:, :, tile_y:], "gy", 1)
        total = total[:, :, :tile_y].at[:, :, 0:1].add(passed_y)
        passed_x = from_behind(total[:, tile_x:], "gx", 1)
        return total[:, :tile_x].at[:, 0:1].add(passed_x)

    def operate(field):
        images = jnp.einsum("nzr,zr->nr", stiffness, spread(field), precision=lax.Precision.HIGHEST)
        return collect(images) + tikhonov * field

    def two_products(vector, image):
        return lax.psum((jnp.sum(vector * vector), jnp.sum(vector * image)), ("gx", "gy"))

    rhs = collect(loads)
    increment = jnp.zeros_like(rhs)
    cg_residual = rhs
    image = operate(cg_residual)
    norm_now, product = two_products(cg_residual, image)
    step_size = norm_now / product
    direction, along = (cg_residual, image)
    for sweep in range(ITERS):
        increment = increment + step_size * direction
        cg_residual = cg_residual - step_size * along
        if sweep + 1 < ITERS:
            image = operate(cg_residual)
            norm_next, product = two_products(cg_residual, image)
            factor = norm_next / norm_now
            step_size = norm_next / (product - factor * norm_next / step_size)
            direction = cg_residual + factor * direction
            along = image + factor * along
            norm_now = norm_next
    return (increment, cg_residual)


def solution(mesh):
    return jax.shard_map(
        per_device,
        mesh=mesh,
        in_specs=(
            P("gx", "gy", None),
            P(None, "gx", "gy", None),
            P("gx", "gy", None),
            P("gx", "gy", None),
            P("gx", "gy", None),
            P("gx", "gy"),
            P(None, "gx", "gy", None),
        ),
        out_specs=(P(None, "gx", "gy", None), P(None, "gx", "gy", None)),
        check_vma=False,
    )
```

profile of v0, /device:TPU:0, one launch (start us, length us, event | category | flops | bytes accessed | tf_op | source)
XLA Modules:
  0.0 903.4 jit_solution(9337056668083446105)
XLA Ops:
  3.0 5.7 collective-permute-start
  13.6 4.5 reshape.733
  18.1 4.5 reshape.734
  22.7 4.0 convert_element_type.286
  26.6 4.2 convert_element_type.287
  30.8 29.1 %scatter_custom_fusion = bf16[8192]{0:T(1024)(128)(2,1)S(1)} fusion(s32[4096]{0:T(1024)S(1)} %bitcast.232, bf16[4096]{0:T(1024)(128)(2,1)S(1)} %fusion.63, bf16[]{:T(256)} %constant.278.clone.1), kind=kCustom, calls=%fused_computation.157 | custom fusion | flops 4096 | bytes 16386 | tf_op jit(solution)/shard_map/scatter-add | solution.py:102
  59.9 10.5 %reshape.725 = bf16[3,8192,128]{2,1,0:T(8,128)(2,1)} reshape(bf16[3,16,32,2048]{3,2,1,0:T(8,128)(2,1)} %param.26) | data formatting | bytes 12582912 | tf_op jit(solution)/shard_map/reshape | solution.py:95
  81.0 6.1 pad_maximum_fusion
  87.1 4.8 copy.263
  91.9 10.6 %reshape.727 = bf16[1092,4,512]{2,1,0:T(4,128)(2,1)} reshape(bf16[26,42,2048]{2,1,0:T(8,128)(2,1)} %copy.263) | data formatting | bytes 8945664 | tf_op jit(solution)/shard_map/reshape | solution.py:81
  102.4 26.4 %gather_fusion = bf16[2048,512]{1,0:T(8,128)(2,1)S(1)} fusion(bf16[1092,4,512]{2,1,0:T(4,128)(2,1)} %reshape.727, s32[2048]{0:T(1024)S(1)} %reshape.737), kind=kCustom, calls=%fused_computation | custom fusion | bytes 4210688 | tf_op jit(solution)/shard_map/gather | solution.py:86
  131.7 26.4 %gather_fusion.1 = bf16[2048,512]{1,0:T(8,128)(2,1)S(1)} fusion(bf16[1092,4,512]{2,1,0:T(4,128)(2,1)} %reshape.727, s32[2048]{0:T(1024)S(1)} %reshape.743), kind=kCustom, calls=%fused_computation.1 | custom fusion | bytes 4210688 | tf_op jit(solution)/shard_map/gather | solution.py:87
  161.0 6.7 subtract_convert_fusion
  167.7 264.3 %while.20 = (s32[]{:T(128)}, f32[4,2048,24,24]{3,2,1,0:T(8,128)}, f32[4,2048,24]{1,2,0:T(8,128)}, s32[4,2048]{1,0:T(4,128)S(1)}, f32[4,8,128]{2,0,1:T(4,128)S(1)...) while((s32[]{:T(128)}, f32[4,2048,24,24]{3,2,1,0:T(8,128)}, ...), condition=%wide.region_2.3_spmd, body=%wide.region_1.2_spmd.sunk | while | flops 434905088 | bytes 179807376 | solution.py:67
  167.9 3.5 fusion.101
  173.0 3.4 multiply_convert_fusion.2
  177.9 6.8 broadcast_multiply_fusion.3
  184.7 27.1 %bitcast_dynamic-update-slice_fusion.4 = f32[4,2048,24,24]{3,2,1,0:T(8,128)} fusion(f32[4,2048,24,24]{3,2,1,0:T(8,128)} %get-tuple-element.346, s32[]{:T(128)} %get-tuple-element.345, bf16[2048,24,128]{2,0,1:T(8,128)(2,1)} %bitcast.212, bf16[2048,24,128]{2,0,1:T(8,128)(2,1)} %broadcast_multiply_fusion.3), kind=kOutput, calls=%fused_computation.3.clone.1 | convolution fusion | flops 301989888 | bytes 50332160 | tf_op jit(solution)/shard_map/while/body/eval_jaxpr/bdv,bev->bde/dot_general | solution.py:53
  211.8 20.8 %fusion.102 = f32[2048,1,24]{2,1,0:T(1,128)S(1)} fusion(bf16[2048,24,128]{2,0,1:T(8,128)(2,1)} %broadcast_multiply_fusion.3, bf16[2048,128,1]{1,0,2:T(8,128)(2,1)S(1)} %dynamic-slice_bitcast_fusion.5), kind=kOutput, calls=%fused_computation.7.clone.1 | convolution fusion | flops 12582912 | bytes 13303808 | tf_op jit(solution)/shard_map/while/body/eval_jaxpr/bdv,bv->bd/dot_general | solution.py:54
  233.8 3.5 fusion.101
  238.9 3.4 multiply_convert_fusion.2
  243.8 6.8 broadcast_multiply_fusion.3
  250.6 27.0 %bitcast_dynamic-update-slice_fusion.4 = f32[4,2048,24,24]{3,2,1,0:T(8,128)} fusion(f32[4,2048,24,24]{3,2,1,0:T(8,128)} %get-tuple-element.346, s32[]{:T(128)} %get-tuple-element.345, bf16[2048,24,128]{2,0,1:T(8,128)(2,1)} %bitcast.212, bf16[2048,24,128]{2,0,1:T(8,128)(2,1)} %broadcast_multiply_fusion.3), kind=kOutput, calls=%fused_computation.3.clone.1 | convolution fusion | flops 301989888 | bytes 50332160 | tf_op jit(solution)/shard_map/while/body/eval_jaxpr/bdv,bev->bde/dot_general | solution.py:53
  277.7 20.8 %fusion.102 = f32[2048,1,24]{2,1,0:T(1,128)S(1)} fusion(bf16[2048,24,128]{2,0,1:T(8,128)(2,1)} %broadcast_multiply_fusion.3, bf16[2048,128,1]{1,0,2:T(8,128)(2,1)S(1)} %dynamic-slice_bitcast_fusion.5), kind=kOutput, calls=%fused_computation.7.clone.1 | convolution fusion | flops 12582912 | bytes 13303808 | tf_op jit(solution)/shard_map/while/body/eval_jaxpr/bdv,bv->bd/dot_general | solution.py:54
  299.7 3.5 fusion.101
  309.7 6.8 broadcast_multiply_fusion.3
  316.5 27.0 %bitcast_dynamic-update-slice_fusion.4 = f32[4,2048,24,24]{3,2,1,0:T(8,128)} fusion(f32[4,2048,24,24]{3,2,1,0:T(8,128)} %get-tuple-element.346, s32[]{:T(128)} %get-tuple-element.345, bf16[2048,24,128]{2,0,1:T(8,128)(2,1)} %bitcast.212, bf16[2048,24,128]{2,0,1:T(8,128)(2,1)} %broadcast_multiply_fusion.3), kind=kOutput, calls=%fused_computation.3.clone.1 | convolution fusion | flops 301989888 | bytes 50332160 | tf_op jit(solution)/shard_map/while/body/eval_jaxpr/bdv,bev->bde/dot_general | solution.py:53
  343.5 20.8 %fusion.102 = f32[2048,1,24]{2,1,0:T(1,128)S(1)} fusion(bf16[2048,24,128]{2,0,1:T(8,128)(2,1)} %broadcast_multiply_fusion.3, bf16[2048,128,1]{1,0,2:T(8,128)(2,1)S(1)} %dynamic-slice_bitcast_fusion.5), kind=kOutput, calls=%fused_computation.7.clone.1 | convolution fusion | flops 12582912 | bytes 13303808 | tf_op jit(solution)/shard_map/while/body/eval_jaxpr/bdv,bv->bd/dot_general | solution.py:54
  365.6 3.5 fusion.101
  375.6 6.8 broadcast_multiply_fusion.3
  382.3 27.1 %bitcast_dynamic-update-slice_fusion.4 = f32[4,2048,24,24]{3,2,1,0:T(8,128)} fusion(f32[4,2048,24,24]{3,2,1,0:T(8,128)} %get-tuple-element.346, s32[]{:T(128)} %get-tuple-element.345, bf16[2048,24,128]{2,0,1:T(8,128)(2,1)} %bitcast.212, bf16[2048,24,128]{2,0,1:T(8,128)(2,1)} %broadcast_multiply_fusion.3), kind=kOutput, calls=%fused_computation.3.clone.1 | convolution fusion | flops 301989888 | bytes 50332160 | tf_op jit(solution)/shard_map/while/body/eval_jaxpr/bdv,bev->bde/dot_general | solution.py:53
  409.5 20.8 %fusion.102 = f32[2048,1,24]{2,1,0:T(1,128)S(1)} fusion(bf16[2048,24,128]{2,0,1:T(8,128)(2,1)} %broadcast_multiply_fusion.3, bf16[2048,128,1]{1,0,2:T(8,128)(2,1)S(1)} %dynamic-slice_bitcast_fusion.5), kind=kOutput, calls=%fused_computation.7.clone.1 | convolution fusion | flops 12582912 | bytes 13303808 | tf_op jit(solution)/shard_map/while/body/eval_jaxpr/bdv,bv->bd/dot_general | solution.py:54
  432.0 3.6 copy.267
  435.5 10.4 %reduce_sum.72 = f32[2048,24]{1,0:T(8,128)S(1)} reduce(f32[2048,4,24]{2,1,0:T(4,128)} %bitcast.215, f32[]{:T(128)} %constant.271.clone.1), dimensions={1}, to_apply=%region_3.4 | reduce | flops 147456 | bytes 983044 | tf_op jit(solution)/shard_map/reduce_sum | solution.py:108
  446.0 4.6 fusion.82
  450.6 5.6 copy.298
  456.2 5.5 copy.299
  461.7 5.5 copy.300
  467.2 5.5 copy.301
  472.7 5.5 copy.302
  478.3 4.3 copy.303
  482.6 3.4 copy.304
  486.0 3.8 copy.305
  493.2 10.1 %collective-permute-start.4 = (f32[3,17,1,5]{3,2,1,0:T(1,128)S(1)}, f32[3,17,1,5]{3,2,1,0:T(1,128)S(1)}, u32[]{:S(2)}, u32[]{:S(2)}) collective-permute-start(f32[3,17,1,5]{3,2,1,0:T(1,128)S(1)} %slice.627), channel_id=1, source_target_pairs={{0,1},{1,2},{2,3},{4,5},{5,6},{6,7},{8,9},{9,10},{10,11},{12,13},{... | collective-permute-start | bytes 3068 | tf_op jit(solution)/shard_map/ppermute | solution.py:27
  504.3 4.6 collective-permute-start.5
  508.9 41.1 %reduce_sum.74 = f32[2048,24,24]{2,1,0:T(8,128)} reduce(f32[2048,4,24,24]{3,2,1,0:T(8,128)} %bitcast.40, f32[]{:T(128)} %constant.271.clone.1), dimensions={1}, to_apply=%region_6.7 | reduce | flops 3538944 | bytes 23592964 | tf_op jit(solution)/shard_map/reduce_sum | solution.py:107
  552.4 3.8 collective-permute-done.6
  565.9 6.7 reshape.728
  572.8 14.2 %fusion.14 = f32[2048,24]{1,0:T(8,128)S(1)} fusion(f32[2048,24,24]{2,1,0:T(8,128)} %reduce_sum.74, f32[2048,24]{1,0:T(8,128)S(1)} %copy.307), kind=kLoop, calls=%fused_computation.24 | loop fusion | flops 2310144 | bytes 5111808
  601.5 4.7 collective-permute-start.8
  607.2 4.5 collective-permute-start.9
  614.4 42.1 %all-reduce.34 = (f32[]{:T(128)}, f32[]{:T(128)}) all-reduce(f32[]{:T(128)} %get-tuple-element.220, f32[]{:T(128)} %get-tuple-element.219), channel_id=1, replica_groups=mesh['gx'=8,'gy'=4] {'gx','gy'}, use_global_device_ids=true, to_apply=%region_5.6 | all-reduce | flops 2 | bytes 16 | tf_op jit(solution)/shard_map/psum | solution.py:143
  660.3 4.0 collective-permute-done.10
  674.0 6.7 reshape.729
  682.0 15.3 %fusion.15 = f32[2048,24]{1,0:T(8,128)} fusion(f32[2048,24,24]{2,1,0:T(8,128)} %reduce_sum.74, f32[2048,24]{1,0:T(8,128)} %copy.308), kind=kLoop, calls=%fused_computation.25 | loop fusion | flops 2310144 | bytes 5111808
  711.6 3.5 pad_add_fusion.1
  715.2 4.6 collective-permute-start.12
  730.0 42.7 %all-reduce.33 = (f32[]{:T(128)}, f32[]{:T(128)}) all-reduce(f32[]{:T(128)} %get-tuple-element.218, f32[]{:T(128)} %get-tuple-element.217), channel_id=1, replica_groups=mesh['gx'=8,'gy'=4] {'gx','gy'}, use_global_device_ids=true, to_apply=%region_10.11 | all-reduce | flops 2 | bytes 16 | tf_op jit(solution)/shard_map/psum | solution.py:143
  781.8 4.0 collective-permute-done.14
  795.6 7.2 reshape.730
  804.1 15.2 %fusion.16 = f32[2048,24]{1,0:T(8,128)} fusion(f32[2048,24,24]{2,1,0:T(8,128)} %reduce_sum.74, f32[2048,24]{1,0:T(8,128)S(1)} %copy.309), kind=kLoop, calls=%fused_computation.26 | loop fusion | flops 2310144 | bytes 5111808
  833.7 3.5 pad_add_fusion
  837.3 4.6 collective-permute-start.16
  850.2 41.9 %all-reduce.32 = (f32[]{:T(128)}, f32[]{:T(128)}) all-reduce(f32[]{:T(128)} %get-tuple-element.216, f32[]{:T(128)} %get-tuple-element.215), channel_id=1, replica_groups=mesh['gx'=8,'gy'=4] {'gx','gy'}, use_global_device_ids=true, to_apply=%region_14.15 | all-reduce | flops 2 | bytes 16 | tf_op jit(solution)/shard_map/psum | solution.py:143
  (202 shorter events, 165.8 us)
Async XLA Ops:
  0.6 12.1 %copy-start.6 = (s32[1,4096]{1,0:T(1,128)S(1)}, s32[1,4096]{1,0:T(1,128)}, u32[]{:S(2)}) copy-start(s32[1,4096]{1,0:T(1,128)} %param.30) | copy-start | bytes 49156
  0.6 12.2 %copy-start.5 = (s32[2,16,32,4]{2,3,1,0:T(4,128)S(1)}, s32[2,16,32,4]{2,3,1,0:T(4,128)}, u32[]{:S(2)}) copy-start(s32[2,16,32,4]{2,3,1,0:T(4,128)} %param.31) | copy-start | bytes 49156
  3.0 67.7 %collective-permute-start = (bf16[5,32,2048]{2,1,0:T(8,128)(2,1)}, bf16[5,32,2048]{2,1,0:T(8,128)(2,1)}, u32[]{:S(2)}, u32[]{:S(2)}) collective-permute-start(bf16[5,32,2048]{2,1,0:T(8,128)(2,1)} %get-tuple-element.249), channel_id=1, source_target_pairs={{0,4},{4,8},{8,12},{12,16},{16,20},{20,24},{24,28},{1,5},{5,9},{9,... | collective-permute-start | bytes 1966088 | tf_op jit(solution)/shard_map/ppermute | solution.py:18
  8.7 63.6 %collective-permute-start.1 = (bf16[5,32,2048]{2,1,0:T(8,128)(2,1)S(1)}, bf16[5,32,2048]{2,1,0:T(8,128)(2,1)}, u32[]{:S(2)}, u32[]{:S(2)}) collective-permute-start(bf16[5,32,2048]{2,1,0:T(8,128)(2,1)S(1)} %get-tuple-element.250), channel_id=1, source_target_pairs={{4,0},{8,4},{12,8},{16,12},{20,16},{24,20},{28,24},{5,1},{9,5},{13... | collective-permute-start | bytes 1966088 | tf_op jit(solution)/shard_map/ppermute | solution.py:19
  70.5 6.5 copy-start.1
  74.2 5.0 collective-permute-start.2
  75.5 5.5 collective-permute-start.3
  176.4 8.3 copy-start
  242.3 8.3 copy-start
  308.2 8.3 copy-start
  374.1 8.3 copy-start
  450.6 27.7 %copy-start.3 = (f32[3,2048]{0,1:T(8,128)S(1)}, f32[3,2048]{0,1:T(8,128)}, u32[]{:S(2)}) copy-start(f32[3,2048]{0,1:T(8,128)} %get-tuple-element.254) | copy-start | bytes 73732
  493.2 10.9 %collective-permute-start.4 = (f32[3,17,1,5]{3,2,1,0:T(1,128)S(1)}, f32[3,17,1,5]{3,2,1,0:T(1,128)S(1)}, u32[]{:S(2)}, u32[]{:S(2)}) collective-permute-start(f32[3,17,1,5]{3,2,1,0:T(1,128)S(1)} %slice.627), channel_id=1, source_target_pairs={{0,1},{1,2},{2,3},{4,5},{5,6},{6,7},{8,9},{9,10},{10,11},{12,13},{... | collective-permute-start | bytes 3068 | tf_op jit(solution)/shard_map/ppermute | solution.py:27
  504.3 45.8 %collective-permute-start.5 = (f32[3,1,32,5]{3,2,1,0:T(8,128)S(1)}, f32[3,1,32,5]{3,2,1,0:T(8,128)S(1)}, u32[]{:S(2)}, u32[]{:S(2)}) collective-permute-start(f32[3,1,32,5]{3,2,1,0:T(8,128)S(1)} %slice.630), channel_id=1, source_target_pairs={{0,4},{4,8},{8,12},{12,16},{16,20},{20,24},{24,28},{1,5},{5,9},{9,... | collective-permute-start | bytes 5768 | tf_op jit(solution)/shard_map/ppermute | solution.py:27
  550.2 6.0 collective-permute-start.6
  556.2 3.1 collective-permute-start.7
  601.5 5.5 collective-permute-start.8
  607.2 6.2 collective-permute-start.9
  658.0 6.2 collective-permute-start.10
  664.3 3.1 collective-permute-start.11
  715.2 5.6 collective-permute-start.12
  723.4 5.0 collective-permute-start.13
  729.1 47.4 %copy-start.2 = (f32[3,16,32,5]{3,2,1,0:T(8,128)}, f32[3,16,32,5]{3,2,1,0:T(8,128)S(1)}, u32[]{:S(2)}) copy-start(f32[3,16,32,5]{3,2,1,0:T(8,128)S(1)} %fusion.51) | copy-start | bytes 92164
  779.6 6.2 collective-permute-start.14
  785.9 3.1 collective-permute-start.15
  837.3 5.5 collective-permute-start.16
  842.9 0.9 copy-start.4
  843.8 4.7 collective-permute-start.17
where the time goes:
time: 914 us; the launch traced here: 903 us
  local copies, waits for them, and re-layouts  260 us (28%)
  other arithmetic  222 us (24%)
  matrix products  205 us (22%)
  blocking collectives  127 us (14%)
  starting transfers between devices  56.9 us (6%)
  waiting for transfers between devices  20.2 us (2%)
  between operations  11.3 us (1%)
    psum x3, blocking collectives, two_products(): lax.psum((jnp.sum(vector * vector), jnp.sum(vector * image)), ('gx', 'gy'))  127 us
    dot_general x4, matrix products, block_terms(): jnp.einsum('bdv,bev->bde', weighted, jacobian, preferred_element_type=jnp...  108 us
    dot_general x4, matrix products, block_terms(): jnp.einsum('bdv,bv->bd', weighted, resid_rows, preferred_element_type=jnp...  83.3 us
    squeeze x32, local copies, waits for them, and re-layouts, collect(): parts[node]  75.9 us
    unnamed x16, other arithmetic  51.3 us
    ppermute x14, starting transfers between devices, from_behind(): return lax.ppermute(block, axis, route)  47.1 us
    reduce_sum x1, other arithmetic, per_device(): elem_hess = hessian.reshape(elements, 4, 24, 24).sum(axis=1)  41.1 us
    scatter-add x1, other arithmetic, per_device(): jnp.zeros((local_blocks,), jnp.bfloat16).at[safe]  29.1 us
  transfers between devices with their start and end apart: 18, of which 13 were waited for; matrix products, arithmetic and copies ran while one was open for 13% of the time, Pallas kernels for 0%

commit v1 on v0

--- a/solution.py
+++ b/solution.py
@@ -140,7 +140,7 @@
         return collect(images) + tikhonov * field
 
     def two_products(vector, image):
-        return lax.psum((jnp.sum(vector * vector), jnp.sum(vector * image)), ("gx", "gy"))
+        return lax.psum(lax.psum((jnp.sum(vector * vector), jnp.sum(vector * image)), "gy"), "gx")
 
     rhs = collect(loads)
     increment = jnp.zeros_like(rhs)

time: 914 us -> 867 us (0.949)
  blocking collectives: 127 us -> 80.5 us
    psum x3 -> x6, blocking collectives: 127 us -> 80.5 us  [the longest x3 61.2 us: two_products(): lax.psum(lax.psum((jnp.sum(vector * vector), jnp.sum(vector * image)), 'g...]
  transfers between devices with their start and end apart: 18 -> 18, of which waited for: 13 -> 13; matrix products, arithmetic and copies ran while one was open for 13% -> 14% of each run, Pallas kernels for 0% -> 0%
where the time goes in v1:
time: 867 us; the launch traced here: 856 us
  local copies, waits for them, and re-layouts  260 us (30%)
  other arithmetic  222 us (26%)
  matrix products  205 us (24%)
  blocking collectives  80.5 us (9%)
  starting transfers between devices  56 us (6%)
  waiting for transfers between devices  19.8 us (2%)
  between operations  11.3 us (1%)
    dot_general x4, matrix products, block_terms(): jnp.einsum('bdv,bev->bde', weighted, jacobian, preferred_element_type=jnp...  108 us
    dot_general x4, matrix products, block_terms(): jnp.einsum('bdv,bv->bd', weighted, resid_rows, preferred_element_type=jnp...  83.3 us
    squeeze x32, local copies, waits for them, and re-layouts, collect(): parts[node]  75.9 us
    psum x3, blocking collectives, two_products(): lax.psum(lax.psum((jnp.sum(vector * vector), jnp.sum(vector * image)), 'g...  61.2 us
    unnamed x16, other arithmetic  51.3 us
    ppermute x14, starting transfers between devices, from_behind(): return lax.ppermute(block, axis, route)  46.2 us
    reduce_sum x1, other arithmetic, per_device(): elem_hess = hessian.reshape(elements, 4, 24, 24).sum(axis=1)  41.1 us
    scatter-add x1, other arithmetic, per_device(): jnp.zeros((local_blocks,), jnp.bfloat16).at[safe]  29.1 us
  transfers between devices with their start and end apart: 18, of which 13 were waited for; matrix products, arithmetic and copies ran while one was open for 14% of the time, Pallas kernels for 0%

profile of v1, /device:TPU:0, one launch (start us, length us, event | category | flops | bytes accessed | tf_op | source)
XLA Modules:
  0.0 856.3 jit_solution(14259471021052187652)
XLA Ops:
  3.0 5.7 collective-permute-start
  13.6 4.5 reshape.733
  18.1 4.5 reshape.734
  22.7 4.0 convert_element_type.286
  26.6 4.2 convert_element_type.287
  30.8 29.1 %scatter_custom_fusion = bf16[8192]{0:T(1024)(128)(2,1)S(1)} fusion(s32[4096]{0:T(1024)S(1)} %bitcast.232, bf16[4096]{0:T(1024)(128)(2,1)S(1)} %fusion.63, bf16[]{:T(256)} %constant.278.clone.1), kind=kCustom, calls=%fused_computation.157 | custom fusion | flops 4096 | bytes 16386 | tf_op jit(solution)/shard_map/scatter-add | solution.py:102
  59.9 10.5 %reshape.725 = bf16[3,8192,128]{2,1,0:T(8,128)(2,1)} reshape(bf16[3,16,32,2048]{3,2,1,0:T(8,128)(2,1)} %param.26) | data formatting | bytes 12582912 | tf_op jit(solution)/shard_map/reshape | solution.py:95
  81.0 6.1 pad_maximum_fusion
  87.1 4.8 copy.263
  91.9 10.6 %reshape.727 = bf16[1092,4,512]{2,1,0:T(4,128)(2,1)} reshape(bf16[26,42,2048]{2,1,0:T(8,128)(2,1)} %copy.263) | data formatting | bytes 8945664 | tf_op jit(solution)/shard_map/reshape | solution.py:81
  102.4 26.4 %gather_fusion = bf16[2048,512]{1,0:T(8,128)(2,1)S(1)} fusion(bf16[1092,4,512]{2,1,0:T(4,128)(2,1)} %reshape.727, s32[2048]{0:T(1024)S(1)} %reshape.737), kind=kCustom, calls=%fused_computation | custom fusion | bytes 4210688 | tf_op jit(solution)/shard_map/gather | solution.py:86
  131.7 26.4 %gather_fusion.1 = bf16[2048,512]{1,0:T(8,128)(2,1)S(1)} fusion(bf16[1092,4,512]{2,1,0:T(4,128)(2,1)} %reshape.727, s32[2048]{0:T(1024)S(1)} %reshape.743), kind=kCustom, calls=%fused_computation.1 | custom fusion | bytes 4210688 | tf_op jit(solution)/shard_map/gather | solution.py:87
  161.0 6.7 subtract_convert_fusion
  167.7 264.3 %while.20 = (s32[]{:T(128)}, f32[4,2048,24,24]{3,2,1,0:T(8,128)}, f32[4,2048,24]{1,2,0:T(8,128)}, s32[4,2048]{1,0:T(4,128)S(1)}, f32[4,8,128]{2,0,1:T(4,128)S(1)...) while((s32[]{:T(128)}, f32[4,2048,24,24]{3,2,1,0:T(8,128)}, ...), condition=%wide.region_2.3_spmd, body=%wide.region_1.2_spmd.sunk | while | flops 434905088 | bytes 179807376 | solution.py:67
  167.9 3.5 fusion.101
  177.9 6.8 broadcast_multiply_fusion.3
  184.7 27.1 %bitcast_dynamic-update-slice_fusion.4 = f32[4,2048,24,24]{3,2,1,0:T(8,128)} fusion(f32[4,2048,24,24]{3,2,1,0:T(8,128)} %get-tuple-element.352, s32[]{:T(128)} %get-tuple-element.351, bf16[2048,24,128]{2,0,1:T(8,128)(2,1)} %bitcast.212, bf16[2048,24,128]{2,0,1:T(8,128)(2,1)} %broadcast_multiply_fusion.3), kind=kOutput, calls=%fused_computation.3.clone.1 | convolution fusion | flops 301989888 | bytes 50332160 | tf_op jit(solution)/shard_map/while/body/eval_jaxpr/bdv,bev->bde/dot_general | solution.py:53
  211.8 20.8 %fusion.102 = f32[2048,1,24]{2,1,0:T(1,128)S(1)} fusion(bf16[2048,24,128]{2,0,1:T(8,128)(2,1)} %broadcast_multiply_fusion.3, bf16[2048,128,1]{1,0,2:T(8,128)(2,1)S(1)} %dynamic-slice_bitcast_fusion.5), kind=kOutput, calls=%fused_computation.7.clone.1 | convolution fusion | flops 12582912 | bytes 13303808 | tf_op jit(solution)/shard_map/while/body/eval_jaxpr/bdv,bv->bd/dot_general | solution.py:54
  233.8 3.5 fusion.101
  243.8 6.8 broadcast_multiply_fusion.3
  250.6 27.0 %bitcast_dynamic-update-slice_fusion.4 = f32[4,2048,24,24]{3,2,1,0:T(8,128)} fusion(f32[4,2048,24,24]{3,2,1,0:T(8,128)} %get-tuple-element.352, s32[]{:T(128)} %get-tuple-element.351, bf16[2048,24,128]{2,0,1:T(8,128)(2,1)} %bitcast.212, bf16[2048,24,128]{2,0,1:T(8,128)(2,1)} %broadcast_multiply_fusion.3), kind=kOutput, calls=%fused_computation.3.clone.1 | convolution fusion | flops 301989888 | bytes 50332160 | tf_op jit(solution)/shard_map/while/body/eval_jaxpr/bdv,bev->bde/dot_general | solution.py:53
  277.7 20.8 %fusion.102 = f32[2048,1,24]{2,1,0:T(1,128)S(1)} fusion(bf16[2048,24,128]{2,0,1:T(8,128)(2,1)} %broadcast_multiply_fusion.3, bf16[2048,128,1]{1,0,2:T(8,128)(2,1)S(1)} %dynamic-slice_bitcast_fusion.5), kind=kOutput, calls=%fused_computation.7.clone.1 | convolution fusion | flops 12582912 | bytes 13303808 | tf_op jit(solution)/shard_map/while/body/eval_jaxpr/bdv,bv->bd/dot_general | solution.py:54
  299.7 3.5 fusion.101
  309.7 6.8 broadcast_multiply_fusion.3
  316.5 27.0 %bitcast_dynamic-update-slice_fusion.4 = f32[4,2048,24,24]{3,2,1,0:T(8,128)} fusion(f32[4,2048,24,24]{3,2,1,0:T(8,128)} %get-tuple-element.352, s32[]{:T(128)} %get-tuple-element.351, bf16[2048,24,128]{2,0,1:T(8,128)(2,1)} %bitcast.212, bf16[2048,24,128]{2,0,1:T(8,128)(2,1)} %broadcast_multiply_fusion.3), kind=kOutput, calls=%fused_computation.3.clone.1 | convolution fusion | flops 301989888 | bytes 50332160 | tf_op jit(solution)/shard_map/while/body/eval_jaxpr/bdv,bev->bde/dot_general | solution.py:53
  343.5 20.8 %fusion.102 = f32[2048,1,24]{2,1,0:T(1,128)S(1)} fusion(bf16[2048,24,128]{2,0,1:T(8,128)(2,1)} %broadcast_multiply_fusion.3, bf16[2048,128,1]{1,0,2:T(8,128)(2,1)S(1)} %dynamic-slice_bitcast_fusion.5), kind=kOutput, calls=%fused_computation.7.clone.1 | convolution fusion | flops 12582912 | bytes 13303808 | tf_op jit(solution)/shard_map/while/body/eval_jaxpr/bdv,bv->bd/dot_general | solution.py:54
  365.6 3.5 fusion.101
  375.6 6.8 broadcast_multiply_fusion.3
  382.3 27.1 %bitcast_dynamic-update-slice_fusion.4 = f32[4,2048,24,24]{3,2,1,0:T(8,128)} fusion(f32[4,2048,24,24]{3,2,1,0:T(8,128)} %get-tuple-element.352, s32[]{:T(128)} %get-tuple-element.351, bf16[2048,24,128]{2,0,1:T(8,128)(2,1)} %bitcast.212, bf16[2048,24,128]{2,0,1:T(8,128)(2,1)} %broadcast_multiply_fusion.3), kind=kOutput, calls=%fused_computation.3.clone.1 | convolution fusion | flops 301989888 | bytes 50332160 | tf_op jit(solution)/shard_map/while/body/eval_jaxpr/bdv,bev->bde/dot_general | solution.py:53
  409.5 20.8 %fusion.102 = f32[2048,1,24]{2,1,0:T(1,128)S(1)} fusion(bf16[2048,24,128]{2,0,1:T(8,128)(2,1)} %broadcast_multiply_fusion.3, bf16[2048,128,1]{1,0,2:T(8,128)(2,1)S(1)} %dynamic-slice_bitcast_fusion.5), kind=kOutput, calls=%fused_computation.7.clone.1 | convolution fusion | flops 12582912 | bytes 13303808 | tf_op jit(solution)/shard_map/while/body/eval_jaxpr/bdv,bv->bd/dot_general | solution.py:54
  432.0 3.6 copy.267
  435.5 10.4 %reduce_sum.72 = f32[2048,24]{1,0:T(8,128)S(1)} reduce(f32[2048,4,24]{2,1,0:T(4,128)} %bitcast.215, f32[]{:T(128)} %constant.271.clone.1), dimensions={1}, to_apply=%region_3.4 | reduce | flops 147456 | bytes 983044 | tf_op jit(solution)/shard_map/reduce_sum | solution.py:108
  446.0 4.6 fusion.82
  450.6 5.6 copy.298
  456.2 5.5 copy.299
  461.7 5.5 copy.300
  467.2 5.5 copy.301
  472.7 5.5 copy.302
  478.3 4.3 copy.303
  486.0 3.8 copy.305
  493.2 10.1 %collective-permute-start.4 = (f32[3,17,1,5]{3,2,1,0:T(1,128)S(1)}, f32[3,17,1,5]{3,2,1,0:T(1,128)S(1)}, u32[]{:S(2)}, u32[]{:S(2)}) collective-permute-start(f32[3,17,1,5]{3,2,1,0:T(1,128)S(1)} %slice.627), channel_id=1, source_target_pairs={{0,1},{1,2},{2,3},{4,5},{5,6},{6,7},{8,9},{9,10},{10,11},{12,13},{... | collective-permute-start | bytes 3068 | tf_op jit(solution)/shard_map/ppermute | solution.py:27
  504.3 4.6 collective-permute-start.5
  508.9 41.1 %reduce_sum.74 = f32[2048,24,24]{2,1,0:T(8,128)} reduce(f32[2048,4,24,24]{3,2,1,0:T(8,128)} %bitcast.40, f32[]{:T(128)} %constant.271.clone.1), dimensions={1}, to_apply=%region_7.8 | reduce | flops 3538944 | bytes 23592964 | tf_op jit(solution)/shard_map/reduce_sum | solution.py:107
  552.4 3.8 collective-permute-done.6
  565.9 6.7 reshape.728
  572.8 14.2 %fusion.14 = f32[2048,24]{1,0:T(8,128)S(1)} fusion(f32[2048,24,24]{2,1,0:T(8,128)} %reduce_sum.74, f32[2048,24]{1,0:T(8,128)S(1)} %copy.307), kind=kLoop, calls=%fused_computation.24 | loop fusion | flops 2310144 | bytes 5111808
  601.5 4.7 collective-permute-start.8
  607.2 4.5 collective-permute-start.9
  614.4 6.5 all-reduce.37
  620.8 21.0 %all-reduce.34 = (f32[]{:T(128)}, f32[]{:T(128)}) all-reduce(f32[]{:T(128)} %get-tuple-element.247, f32[]{:T(128)} %get-tuple-element.248), channel_id=1, replica_groups=mesh['gx'=8,'gy'=4] {'gx'}, use_global_device_ids=true, to_apply=%region_6.7 | all-reduce | flops 2 | bytes 16 | tf_op jit(solution)/shard_map/psum | solution.py:143
  645.6 3.8 collective-permute-done.10
  659.1 6.8 reshape.729
  667.2 15.3 %fusion.15 = f32[2048,24]{1,0:T(8,128)} fusion(f32[2048,24,24]{2,1,0:T(8,128)} %reduce_sum.74, f32[2048,24]{1,0:T(8,128)} %copy.308), kind=kLoop, calls=%fused_computation.25 | loop fusion | flops 2310144 | bytes 5111808
  696.9 3.5 pad_add_fusion.1
  700.4 4.6 collective-permute-start.12
  715.1 6.3 all-reduce.36
  721.5 20.1 %all-reduce.33 = (f32[]{:T(128)}, f32[]{:T(128)}) all-reduce(f32[]{:T(128)} %get-tuple-element.245, f32[]{:T(128)} %get-tuple-element.246), channel_id=1, replica_groups=mesh['gx'=8,'gy'=4] {'gx'}, use_global_device_ids=true, to_apply=%region_13.14 | all-reduce | flops 2 | bytes 16 | tf_op jit(solution)/shard_map/psum | solution.py:143
  750.8 3.8 collective-permute-done.14
  764.2 7.4 reshape.730
  772.9 15.2 %fusion.16 = f32[2048,24]{1,0:T(8,128)} fusion(f32[2048,24,24]{2,1,0:T(8,128)} %reduce_sum.74, f32[2048,24]{1,0:T(8,128)S(1)} %copy.309), kind=kLoop, calls=%fused_computation.26 | loop fusion | flops 2310144 | bytes 5111808
  802.6 3.5 pad_add_fusion
  806.1 4.6 collective-permute-start.16
  818.5 6.5 all-reduce.35
  825.0 20.1 %all-reduce.32 = (f32[]{:T(128)}, f32[]{:T(128)}) all-reduce(f32[]{:T(128)} %get-tuple-element.243, f32[]{:T(128)} %get-tuple-element.244), channel_id=1, replica_groups=mesh['gx'=8,'gy'=4] {'gx'}, use_global_device_ids=true, to_apply=%region_19.20 | all-reduce | flops 2 | bytes 16 | tf_op jit(solution)/shard_map/psum | solution.py:143
  (205 shorter events, 175.3 us)
Async XLA Ops:
  0.6 12.1 %copy-start.6 = (s32[1,4096]{1,0:T(1,128)S(1)}, s32[1,4096]{1,0:T(1,128)}, u32[]{:S(2)}) copy-start(s32[1,4096]{1,0:T(1,128)} %param.30) | copy-start | bytes 49156
  0.6 12.2 %copy-start.5 = (s32[2,16,32,4]{2,3,1,0:T(4,128)S(1)}, s32[2,16,32,4]{2,3,1,0:T(4,128)}, u32[]{:S(2)}) copy-start(s32[2,16,32,4]{2,3,1,0:T(4,128)} %param.31) | copy-start | bytes 49156
  3.0 67.7 %collective-permute-start = (bf16[5,32,2048]{2,1,0:T(8,128)(2,1)}, bf16[5,32,2048]{2,1,0:T(8,128)(2,1)}, u32[]{:S(2)}, u32[]{:S(2)}) collective-permute-start(bf16[5,32,2048]{2,1,0:T(8,128)(2,1)} %get-tuple-element.255), channel_id=1, source_target_pairs={{0,4},{4,8},{8,12},{12,16},{16,20},{20,24},{24,28},{1,5},{5,9},{9,... | collective-permute-start | bytes 1966088 | tf_op jit(solution)/shard_map/ppermute | solution.py:18
  8.7 63.6 %collective-permute-start.1 = (bf16[5,32,2048]{2,1,0:T(8,128)(2,1)S(1)}, bf16[5,32,2048]{2,1,0:T(8,128)(2,1)}, u32[]{:S(2)}, u32[]{:S(2)}) collective-permute-start(bf16[5,32,2048]{2,1,0:T(8,128)(2,1)S(1)} %get-tuple-element.256), channel_id=1, source_target_pairs={{4,0},{8,4},{12,8},{16,12},{20,16},{24,20},{28,24},{5,1},{9,5},{13... | collective-permute-start | bytes 1966088 | tf_op jit(solution)/shard_map/ppermute | solution.py:19
  70.5 6.5 copy-start.1
  74.2 5.0 collective-permute-start.2
  75.5 5.5 collective-permute-start.3
  176.4 8.3 copy-start
  242.3 8.3 copy-start
  308.2 8.3 copy-start
  374.1 8.3 copy-start
  450.6 27.7 %copy-start.3 = (f32[3,2048]{0,1:T(8,128)S(1)}, f32[3,2048]{0,1:T(8,128)}, u32[]{:S(2)}) copy-start(f32[3,2048]{0,1:T(8,128)} %get-tuple-element.260) | copy-start | bytes 73732
  493.2 10.9 %collective-permute-start.4 = (f32[3,17,1,5]{3,2,1,0:T(1,128)S(1)}, f32[3,17,1,5]{3,2,1,0:T(1,128)S(1)}, u32[]{:S(2)}, u32[]{:S(2)}) collective-permute-start(f32[3,17,1,5]{3,2,1,0:T(1,128)S(1)} %slice.627), channel_id=1, source_target_pairs={{0,1},{1,2},{2,3},{4,5},{5,6},{6,7},{8,9},{9,10},{10,11},{12,13},{... | collective-permute-start | bytes 3068 | tf_op jit(solution)/shard_map/ppermute | solution.py:27
  504.3 45.8 %collective-permute-start.5 = (f32[3,1,32,5]{3,2,1,0:T(8,128)S(1)}, f32[3,1,32,5]{3,2,1,0:T(8,128)S(1)}, u32[]{:S(2)}, u32[]{:S(2)}) collective-permute-start(f32[3,1,32,5]{3,2,1,0:T(8,128)S(1)} %slice.630), channel_id=1, source_target_pairs={{0,4},{4,8},{8,12},{12,16},{16,20},{20,24},{24,28},{1,5},{5,9},{9,... | collective-permute-start | bytes 5768 | tf_op jit(solution)/shard_map/ppermute | solution.py:27
  550.2 6.0 collective-permute-start.6
  556.2 3.1 collective-permute-start.7
  601.5 5.5 collective-permute-start.8
  607.2 6.2 collective-permute-start.9
  643.4 6.0 collective-permute-start.10
  649.4 3.1 collective-permute-start.11
  700.4 5.6 collective-permute-start.12
  708.6 4.7 collective-permute-start.13
  714.1 31.4 %copy-start.2 = (f32[3,16,32,5]{3,2,1,0:T(8,128)}, f32[3,16,32,5]{3,2,1,0:T(8,128)S(1)}, u32[]{:S(2)}) copy-start(f32[3,16,32,5]{3,2,1,0:T(8,128)S(1)} %fusion.51) | copy-start | bytes 92164
  748.5 6.0 collective-permute-start.14
  754.5 3.1 collective-permute-start.15
  806.1 5.4 collective-permute-start.16
  811.7 0.9 copy-start.4
  812.6 4.2 collective-permute-start.17
